TPU v7x, 128 devices: a whole 4x4x4 slice. The times are simulated.
128 devices in a mesh: blk: 16 (over x_hi, z, core), uly: 8 (over x_lo, y).
Axes of the slice: x: 4 (x_hi: 2, x_lo: 2; x = x_hi * 2 + x_lo), y: 4, z: 4, core: 2. Of those that a mesh axis runs over, the one named last changes fastest.
Arguments:
- queries: bfloat16 [32768, 4096], P(('blk', 'uly')), may hold values from -140 to 140
- keys: bfloat16 [32768, 1024], P(('blk', 'uly')), may hold values from -6 to 6
- values: bfloat16 [32768, 1024], P(('blk', 'uly')), may hold values from -6 to 6
- doc_lengths: int32 [4], replicated, may hold values from 1 to 24576, 32768 in all
- selected: int32 [32, 8], replicated, may hold values from 0 to 30, as said below
Outputs:
- attended: bfloat16 [32768, 4096], P(('blk', 'uly'))
Inputs may be any that keep to these rules, and one draw needn't show every extreme that they name: selected[b, g] <= b, and equals b only for b = 0. For every device index along blk (blocks b with equal b // 2) and every key head, the blocks it selects that lie outside its own 2 blocks lie in distinct blocks of blk, so one other index of blk supplies at most one selected block a key head to it.
All inputs are finite; a program needn't handle non-finite values.
Results may differ from a plain program's by a relative error of at most 0.004.
Values may be sent and summed in bfloat16 or wider, within the bound.
A program may use at most 128 MiB of HBM per device.

v0:
```python
import jax
import jax.numpy as jnp
from jax import lax
from jax.sharding import PartitionSpec as P

HQ = 32
KVH = 8
HD = 128
MB = 1024


def shortened(shard):

    def short(part):
        return part.astype(jnp.bfloat16) if part.dtype == jnp.float32 else part

    return jax.tree.map(short, shard)


def on_device(queries, keys, values, doc_lengths, selected):
    q_heads, k_heads, v_heads = (
        lax.all_to_all(queries, "uly", split_axis=1, concat_axis=0, tiled=True),
        lax.all_to_all(keys, "uly", split_axis=1, concat_axis=0, tiled=True),
        lax.all_to_all(values, "uly", split_axis=1, concat_axis=0, tiled=True),
    )
    shard = k_heads.shape[0]
    kv_dev = k_heads.shape[1] // HD
    per_dev = shard // MB
    group = HQ // KVH
    scale = 1.0 / HD**0.5
    blk_index = lax.axis_index("blk")
    uly_index = lax.axis_index("uly")
    ends = jnp.cumsum(doc_lengths)

    def doc_of(places):
        return jnp.sum((ends <= places[..., None]).astype(jnp.int32), axis=-1)

    column = lax.dynamic_slice_in_dim(selected, uly_index * kv_dev, kv_dev, 1)
    mine = lax.dynamic_slice_in_dim(column, blk_index * per_dev, per_dev, 0)
    offsets = jnp.arange(MB, dtype=jnp.int32)
    k_blocks = k_heads.reshape(per_dev, MB, kv_dev, HD)
    v_blocks = v_heads.reshape(per_dev, MB, kv_dev, HD)
    empty = jnp.zeros((per_dev, kv_dev, MB, HD), jnp.bfloat16)
    k_piece = lax.all_gather(k_heads, "blk", axis=0, tiled=True)
    v_piece = lax.all_gather(v_heads, "blk", axis=0, tiled=True)
    count = k_piece.shape[0]
    wanted_rows = mine[:, :, None] * MB + offsets
    inside = (wanted_rows >= 0) & (wanted_rows < count)
    index = jnp.clip(wanted_rows, 0, count - 1)
    head_rows = jnp.arange(kv_dev, dtype=jnp.int32)[None, :, None]
    k_got = k_piece.reshape(count, kv_dev, HD)[index, head_rows]
    v_got = v_piece.reshape(count, kv_dev, HD)[index, head_rows]
    chosen_k = jnp.where(inside[..., None], k_got, empty)
    chosen_v = jnp.where(inside[..., None], v_got, empty)
    doc_query = doc_of(blk_index * shard + jnp.arange(shard, dtype=jnp.int32)).reshape(per_dev, MB)
    doc_chosen = doc_of(mine[:, :, None] * MB + offsets)
    live = mine != (blk_index * per_dev + jnp.arange(per_dev, dtype=jnp.int32))[:, None]
    q_five = q_heads.reshape(per_dev, MB, kv_dev, group, HD)
    causal = offsets[:, None] >= offsets[None, :]

    def one_block(row):
        q_now = q_five[row, :, 0]
        own_k = k_blocks[row, :, 0]
        own_v = v_blocks[row, :, 0]
        doc_now = doc_query[row]
        own_scores = (
            jnp.einsum("mgd,nd->gmn", q_now, own_k, preferred_element_type=jnp.float32) * scale
        )
        sel_scores = (
            jnp.einsum("mgd,nd->gmn", q_now, chosen_k[row, 0], preferred_element_type=jnp.float32)
            * scale
        )
        own_mask = causal & (doc_now[:, None] == doc_now[None, :])
        sel_mask = (doc_now[:, None] == doc_chosen[row, 0][None, :]) & live[row, 0]
        top = jnp.maximum(
            jnp.max(jnp.where(own_mask, own_scores, -jnp.inf), axis=-1),
            jnp.max(jnp.where(sel_mask, sel_scores, -jnp.inf), axis=-1),
        )
        own_weight = jnp.where(own_mask, jnp.exp(own_scores - top[..., None]), 0.0)
        sel_weight = jnp.where(sel_mask, jnp.exp(sel_scores - top[..., None]), 0.0)
        total = jnp.sum(own_weight, axis=-1) + jnp.sum(sel_weight, axis=-1)
        acc = jnp.einsum(
            "gmn,nd->mgd",
            own_weight.astype(jnp.bfloat16),
            own_v,
            preferred_element_type=jnp.float32,
        )
        acc = acc + jnp.einsum(
            "gmn,nd->mgd",
            sel_weight.astype(jnp.bfloat16),
            chosen_v[row, 0],
            preferred_element_type=jnp.float32,
        )
        output = (acc / jnp.transpose(total)[:, :, None]).astype(jnp.bfloat16)
        results = [output.reshape(MB, group * HD)]
        return jnp.concatenate(results, axis=1)

    blocks = lax.map(one_block, jnp.arange(per_dev, dtype=jnp.int32))
    head_major = blocks.reshape(shard, kv_dev * group * HD)
    return lax.all_to_all(
        shortened(head_major), "uly", split_axis=0, concat_axis=1, tiled=True
    ).astype(head_major.dtype)


def solution(mesh):
    placed = (P(("blk", "uly"), None), P(("blk", "uly"), None), P(("blk", "uly"), None), P(), P())
    return jax.shard_map(
        on_device, mesh=mesh, in_specs=placed, out_specs=P(("blk", "uly"), None), check_vma=False
    )
```

profile of v0, /device:TPU:1, one launch (start us, length us, event | category | flops | bytes accessed | tf_op | source)
XLA Modules:
  0.0 338.5 jit_solution(10035589432104716026)
XLA Ops:
  6.5 1.3 copy.43
  7.8 14.4 %all_to_all.73 = bf16[256,8,128]{0,2,1:T(8,128)(2,1)S(1)} all-to-all(bf16[256,8,128]{0,2,1:T(8,128)(2,1)S(1)} %bitcast.166), channel_id=1, replica_groups=mesh['blk'=16,'uly'=8] {'uly'}, dimensions={1} | all-to-all | bytes 1048576 | tf_op jit(solution)/shard_map/all_to_all | solution.py:24
  22.2 1.0 copy.44
  23.3 0.1 copy_bitcast_fusion.4
  23.4 10.6 %all_to_all.74 = bf16[256,8,128]{2,0,1:T(8,128)(2,1)} all-to-all(bf16[256,8,128]{2,0,1:T(8,128)(2,1)S(1)} %copy_bitcast_fusion.4), channel_id=1, replica_groups=mesh['blk'=16,'uly'=8] {'uly'}, dimensions={1} | all-to-all | bytes 1048576 | tf_op jit(solution)/shard_map/all_to_all | solution.py:23
  34.0 3.3 copy.80
  37.3 3.6 %all-to-all-start.2 = ((bf16[256,8,512]{2,0,1:T(8,128)(2,1)}), bf16[256,8,512]{2,0,1:T(8,128)(2,1)S(1)}, u32[]{:S(2)}, u32[]{:S(2)}) async-start(bf16[256,8,512]{2,0,1:T(8,128)(2,1)} %bitcast.154), calls=%async_computation.2 | async-start | bytes 4194304 | tf_op jit(solution)/shard_map/all_to_all | solution.py:22
  41.0 0.8 dynamic_slice.32
  41.7 0.1 copy.66
  41.8 0.1 multiply_reduce_fusion
  42.1 0.8 reduce-window.8
  42.9 0.1 convert_reduce_fusion.1
  43.1 0.1 convert_reduce_fusion
  43.3 22.7 %all-to-all-done.2 = bf16[256,8,512]{2,0,1:T(8,128)(2,1)S(1)} async-done(((bf16[256,8,512]{2,0,1:T(8,128)(2,1)}), bf16[256,8,512]{2,0,1:T(8,128)(2,1)S(1)}, u32[]{:S(2)}, u32[]{:S(2)}) %all-to-all-start.2) | async-done | bytes 2097184 | tf_op jit(solution)/shard_map/all_to_all | solution.py:22
  66.0 2.1 reshape.225
  68.1 34.9 %all-gather.5.cloned.1.call-done = bf16[32768,128]{1,0:T(8,128)(2,1)} async-done(((bf16[2048,128]{1,0:T(8,128)(2,1)}), bf16[32768,128]{1,0:T(8,128)(2,1)}) %all-gather.5.cloned.1.call-update) | async-done | bytes 8388624 | tf_op jit(solution)/shard_map/all_gather | solution.py:45
  103.0 22.7 %gather_fusion.1 = bf16[2048,128]{1,0:T(8,128)(2,1)S(1)} fusion(bf16[32768,1,128]{2,0,1:T(8,128)(2,1)} %bitcast.157, s32[2048]{0:T(1024)S(1)} %bitcast.150), kind=kCustom, calls=%fused_computation.1 | custom fusion | bytes 1064960 | tf_op jit(solution)/shard_map/gather | solution.py:52
  125.6 0.2 copy.50
  125.8 50.9 %all-gather.3.cloned.1.call-done = bf16[32768,128]{1,0:T(8,128)(2,1)} async-done(((bf16[2048,128]{1,0:T(8,128)(2,1)}), bf16[32768,128]{1,0:T(8,128)(2,1)}) %all-gather.3.cloned.1.call-update) | async-done | bytes 8388624 | tf_op jit(solution)/shard_map/all_gather | solution.py:44
  176.8 22.5 %gather_fusion = bf16[2048,128]{1,0:T(8,128)(2,1)S(1)} fusion(bf16[32768,1,128]{2,0,1:T(8,128)(2,1)} %bitcast.158, s32[2048]{0:T(1024)S(1)} %bitcast.151), kind=kCustom, calls=%fused_computation | custom fusion | bytes 1064960 | tf_op jit(solution)/shard_map/gather | solution.py:51
  199.3 0.2 copy.48
  199.5 1.1 broadcast_select_fusion
  200.6 94.8 %while.11 = (s32[]{:T(128)}, bf16[2,1024,512]{2,1,0:T(8,128)(2,1)}, s32[2]{0:T(128)S(1)}, bf16[2,1024,1,128]{3,1,0,2:T(8,128)(2,1)S(1)}, s32[2,1024]{1,0:T(2,128...) while((s32[]{:T(128)}, bf16[2,1024,512]{2,1,0:T(8,128)(2,1)}, ...), condition=%wide.region_8.9_spmd.clone, body=%wide.region_3.8_spmd.clone.sunk | while | flops 4394049536 | bytes 123986648 | solution.py:98
  200.6 0.6 dynamic_slice.83
  203.1 0.6 constant_dynamic-slice_fusion.10
  203.6 2.5 compare_and_fusion.3
  206.1 1.6 constant_dynamic-slice_fusion.11
  207.7 4.0 %fusion.59 = (f32[4,1024]{1,0:T(4,128)S(1)}, f32[1024,1024,4]{1,0,2:T(8,128)S(1)}) fusion(pred[1024,1024]{0,1:T(8,128)(4,1)S(1)} %get-tuple-element.245, bf16[1,1024,1,4,128]{4,3,1,0,2:T(4,128)(2,1)S(1)} %constant_dynamic-slice_fusion.11, bf16[2,1024,1,128]{3,1,2,0:T(8,128)(2,1)} %get-tuple-element.284, s32[]{:T(128)S(6)} %select_n.115), kind=kOutput, calls=%fused_computation.10.clone.1 | convolution fusion | flops 1086320640 | bytes 19152900 | tf_op jit(solution)/shard_map/while/body/eval_jaxpr/mgd,nd->gmn/dot_general | solution.py:67
  211.7 8.5 %fusion.58 = (f32[4,1024]{1,0:T(4,128)S(1)}, f32[1024,1024,4]{1,0,2:T(8,128)}) fusion(pred[1024,1024]{0,1:T(8,128)(4,1)S(1)} %get-tuple-element.243, bf16[1,1024,1,4,128]{4,3,1,0,2:T(4,128)(2,1)S(1)} %constant_dynamic-slice_fusion.11, bf16[2,1,1024,128]{2,3,1,0:T(8,128)(2,1)} %get-tuple-element.288, s32[]{:T(128)S(6)} %select_n.115), kind=kOutput, calls=%fused_computation.5.clone.1 | convolution fusion | flops 1086320640 | bytes 19152900 | tf_op jit(solution)/shard_map/while/body/eval_jaxpr/mgd,nd->gmn/dot_general | solution.py:70
  220.2 9.9 %fusion.61 = (f32[4,1024]{1,0:T(4,128)S(1)}, f32[4,1024]{1,0:T(4,128)S(1)}) fusion(f32[1024,1024,4]{1,0,2:T(8,128)} %get-tuple-element.244, f32[4,1024]{1,0:T(4,128)S(1)} %max.13, pred[1024,1024]{0,1:T(8,128)(4,1)S(1)} %get-tuple-element.243, f32[1024,1024,4]{1,0,2:T(8,128)S(1)} %get-tuple-element.248, pred[1024,1024]{0,1:T(8,128)(4,1)S(1)} %get-tuple-element.245), kind=kLoop, calls=%fused_computation.15.clone.1 | loop fusion | flops 33546240 | bytes 35700736 | tf_op jit(solution)/shard_map/while/body/eval_jaxpr/reduce_sum | solution.py:81
  230.2 11.0 %fusion.60 = f32[128,4,1024]{2,0,1:T(8,128)} fusion(f32[1024,1024,4]{1,0,2:T(8,128)} %get-tuple-element.244, f32[4,1024]{1,0:T(4,128)S(1)} %max.13, pred[1024,1024]{0,1:T(8,128)(4,1)S(1)} %get-tuple-element.243, bf16[2,1,1024,128]{2,3,1,0:T(8,128)(2,1)} %get-tuple-element.289, s32[]{:T(128)S(6)} %select_n.115), kind=kOutput, calls=%fused_computation.17.clone.1 | convolution fusion | flops 1090519040 | bytes 20201476 | tf_op jit(solution)/shard_map/while/body/eval_jaxpr/gmn,nd->mgd/dot_general | solution.py:88
  241.1 5.2 %fusion.62 = bf16[1024,4,128]{0,2,1:T(8,128)(2,1)S(1)} fusion(f32[128,4,1024]{2,0,1:T(8,128)} %fusion.60, f32[1024,1024,4]{1,0,2:T(8,128)S(1)} %get-tuple-element.248, f32[4,1024]{1,0:T(4,128)S(1)} %max.13, pred[1024,1024]{0,1:T(8,128)(4,1)S(1)} %get-tuple-element.245, f32[1024,4]{0,1:T(4,128)S(1)} %add_bitcast_fusion.2, ...), kind=kOutput, calls=%fused_computation.25.clone.1 | convolution fusion | flops 1092091904 | bytes 21266436 | tf_op jit(solution)/shard_map/while/body/eval_jaxpr/gmn,nd->mgd/dot_general | solution.py:82
  246.4 0.5 copy.87
  246.9 1.0 constant_dynamic-update-slice_fusion.2
  248.0 0.6 dynamic_slice.83
  250.5 0.6 constant_dynamic-slice_fusion.10
  251.0 2.5 compare_and_fusion.3
  253.5 1.6 constant_dynamic-slice_fusion.11
  255.1 4.0 %fusion.59 = (f32[4,1024]{1,0:T(4,128)S(1)}, f32[1024,1024,4]{1,0,2:T(8,128)S(1)}) fusion(pred[1024,1024]{0,1:T(8,128)(4,1)S(1)} %get-tuple-element.245, bf16[1,1024,1,4,128]{4,3,1,0,2:T(4,128)(2,1)S(1)} %constant_dynamic-slice_fusion.11, bf16[2,1024,1,128]{3,1,2,0:T(8,128)(2,1)} %get-tuple-element.284, s32[]{:T(128)S(6)} %select_n.115), kind=kOutput, calls=%fused_computation.10.clone.1 | convolution fusion | flops 1086320640 | bytes 19152900 | tf_op jit(solution)/shard_map/while/body/eval_jaxpr/mgd,nd->gmn/dot_general | solution.py:67
  259.1 8.5 %fusion.58 = (f32[4,1024]{1,0:T(4,128)S(1)}, f32[1024,1024,4]{1,0,2:T(8,128)}) fusion(pred[1024,1024]{0,1:T(8,128)(4,1)S(1)} %get-tuple-element.243, bf16[1,1024,1,4,128]{4,3,1,0,2:T(4,128)(2,1)S(1)} %constant_dynamic-slice_fusion.11, bf16[2,1,1024,128]{2,3,1,0:T(8,128)(2,1)} %get-tuple-element.288, s32[]{:T(128)S(6)} %select_n.115), kind=kOutput, calls=%fused_computation.5.clone.1 | convolution fusion | flops 1086320640 | bytes 19152900 | tf_op jit(solution)/shard_map/while/body/eval_jaxpr/mgd,nd->gmn/dot_general | solution.py:70
  267.6 9.9 %fusion.61 = (f32[4,1024]{1,0:T(4,128)S(1)}, f32[4,1024]{1,0:T(4,128)S(1)}) fusion(f32[1024,1024,4]{1,0,2:T(8,128)} %get-tuple-element.244, f32[4,1024]{1,0:T(4,128)S(1)} %max.13, pred[1024,1024]{0,1:T(8,128)(4,1)S(1)} %get-tuple-element.243, f32[1024,1024,4]{1,0,2:T(8,128)S(1)} %get-tuple-element.248, pred[1024,1024]{0,1:T(8,128)(4,1)S(1)} %get-tuple-element.245), kind=kLoop, calls=%fused_computation.15.clone.1 | loop fusion | flops 33546240 | bytes 35700736 | tf_op jit(solution)/shard_map/while/body/eval_jaxpr/reduce_sum | solution.py:81
  277.6 11.0 %fusion.60 = f32[128,4,1024]{2,0,1:T(8,128)} fusion(f32[1024,1024,4]{1,0,2:T(8,128)} %get-tuple-element.244, f32[4,1024]{1,0:T(4,128)S(1)} %max.13, pred[1024,1024]{0,1:T(8,128)(4,1)S(1)} %get-tuple-element.243, bf16[2,1,1024,128]{2,3,1,0:T(8,128)(2,1)} %get-tuple-element.289, s32[]{:T(128)S(6)} %select_n.115), kind=kOutput, calls=%fused_computation.17.clone.1 | convolution fusion | flops 1090519040 | bytes 20201476 | tf_op jit(solution)/shard_map/while/body/eval_jaxpr/gmn,nd->mgd/dot_general | solution.py:88
  288.5 5.2 %fusion.62 = bf16[1024,4,128]{0,2,1:T(8,128)(2,1)S(1)} fusion(f32[128,4,1024]{2,0,1:T(8,128)} %fusion.60, f32[1024,1024,4]{1,0,2:T(8,128)S(1)} %get-tuple-element.248, f32[4,1024]{1,0:T(4,128)S(1)} %max.13, pred[1024,1024]{0,1:T(8,128)(4,1)S(1)} %get-tuple-element.245, f32[1024,4]{0,1:T(4,128)S(1)} %add_bitcast_fusion.2, ...), kind=kOutput, calls=%fused_computation.25.clone.1 | convolution fusion | flops 1092091904 | bytes 21266436 | tf_op jit(solution)/shard_map/while/body/eval_jaxpr/gmn,nd->mgd/dot_general | solution.py:82
  293.8 0.5 copy.87
  294.3 1.0 constant_dynamic-update-slice_fusion.2
  295.4 29.8 %all_to_all.75 = bf16[8,256,512]{2,1,0:T(8,128)(2,1)S(1)} all-to-all(bf16[8,256,512]{2,1,0:T(8,128)(2,1)} %bitcast.160), channel_id=1, replica_groups=mesh['blk'=16,'uly'=8] {'uly'}, dimensions={0} | all-to-all | bytes 4194304 | tf_op jit(solution)/shard_map/all_to_all | solution.py:100
  325.2 2.4 copy.56
  327.6 4.1 %copy.57 = bf16[256,4096]{1,0:T(8,128)(2,1)} copy(bf16[256,4096]{0,1:T(8,128)(2,1)} %bitcast.156) | data formatting | bytes 4194304 | tf_op jit(solution)/shard_map/all_to_all | solution.py:100
  (29 shorter events, 0.4 us)
Async XLA Ops:
  6.5 16.8 %copy-start = (bf16[256,1024]{1,0:T(8,128)(2,1)S(1)}, bf16[256,1024]{1,0:T(8,128)(2,1)}, u32[]{:S(2)}) copy-start(bf16[256,1024]{1,0:T(8,128)(2,1)} %param.8) | copy-start | bytes 1572868
  6.5 96.4 %all-gather.5.cloned.1.call-start = ((), (), s32[]{:S(2)}) async-start(), calls=%async_computation.5 | async-start | bytes 8912896 | tf_op jit(solution)/shard_map/all_gather | solution.py:45
  23.2 177.4 %copy-start.2 = (bf16[8,256,128]{2,1,0:T(8,128)(2,1)S(1)}, bf16[8,256,128]{2,1,0:T(8,128)(2,1)}, u32[]{:S(2)}) copy-start(bf16[8,256,128]{2,1,0:T(8,128)(2,1)} %copy.44) | copy-start | bytes 1572868
  23.2 153.5 %all-gather.3.cloned.1.call-start = ((), (), s32[]{:S(2)}) async-start(), calls=%async_computation.4 | async-start | bytes 8912896 | tf_op jit(solution)/shard_map/all_gather | solution.py:44
  37.3 28.7 %all-to-all-start.2 = ((bf16[256,8,512]{2,0,1:T(8,128)(2,1)}), bf16[256,8,512]{2,0,1:T(8,128)(2,1)S(1)}, u32[]{:S(2)}, u32[]{:S(2)}) async-start(bf16[256,8,512]{2,0,1:T(8,128)(2,1)} %bitcast.154), calls=%async_computation.2 | async-start | bytes 4194304 | tf_op jit(solution)/shard_map/all_to_all | solution.py:22
  295.4 36.2 %copy-start.1 = (bf16[256,1024]{1,0:T(8,128)(2,1)S(1)}, bf16[256,1024]{1,0:T(8,128)(2,1)}, u32[]{:S(2)}) copy-start(bf16[256,1024]{1,0:T(8,128)(2,1)} %param.8) | copy-start | bytes 1572868
Sparse Core Ops, SparseCore 0:
  23.4 79.5 all-gather.4
  105.4 71.2 all-gather.2
where the time goes:
time: 341 us; the launch traced here: 338 us
  waiting for transfers between devices  109 us (32%)
  local copies, waits for them, and re-layouts  69.4 us (20%)
  matrix products  57.4 us (17%)
  blocking collectives  54.8 us (16%)
  other arithmetic  27.3 us (8%)
  between operations  13.5 us (4%)
  loops' own time  3.8 us (1%)
  starting transfers between devices  3.65 us (1%)
    all_gather x1, waiting for transfers between devices, on_device(): k_piece = lax.all_gather(k_heads, 'blk', axis=0, tiled=True)  50.9 us
    all_gather x1, waiting for transfers between devices, on_device(): v_piece = lax.all_gather(v_heads, 'blk', axis=0, tiled=True)  34.9 us
    all_to_all x1, blocking collectives, on_device(): lax.all_to_all(shortened(head_major), 'uly', split_axis=0, concat_axis=1,...  29.8 us
    gather x2, local copies, waits for them, and re-layouts, on_device(): v_got = v_piece.reshape(count, kv_dev, HD)[index, head_rows]  22.9 us
    gather x2, local copies, waits for them, and re-layouts, on_device(): k_got = k_piece.reshape(count, kv_dev, HD)[index, head_rows]  22.7 us
    all_to_all x1, waiting for transfers between devices, on_device(): lax.all_to_all(queries, 'uly', split_axis=1, concat_axis=0, tiled=True)  22.7 us
    dot_general x2, matrix products, one_block(): jnp.einsum('gmn,nd->mgd', sel_weight.astype(jnp.bfloat16), chosen_v[row,...  21.9 us
    reduce_sum x2, other arithmetic, one_block(): total = jnp.sum(own_weight, axis=-1) + jnp.sum(sel_weight, axis=-1)  19.9 us
  transfers between devices with their start and end apart: 3, of which 3 were waited for; matrix products, arithmetic and copies ran while one was open for 9% of the time, Pallas kernels for 0%

commit v1 on v0

v1 whole, which is shorter than its diff:
```python
import functools
import math

import jax
import jax.numpy as jnp
from jax import lax
from jax.experimental import pallas as pl
from jax.experimental.pallas import tpu as pltpu
from jax.sharding import PartitionSpec as P

HQ = 32
KVH = 8
HD = 128
NY = 4
GROUP = HQ // KVH
HEADS = KVH // NY
BIG = float(1 << 20)
LOG2E_SCALE = math.log2(math.e) / math.sqrt(HD)
MESH = pl.DeviceIdType.MESH


def device(x, y, z, c):
    return ((x // 2) * 8 + z * 2 + c, (x % 2) * NY + y)


def kernel(
    rows,
    q_hbm,
    k_hbm,
    v_hbm,
    lengths,
    selected,
    out_hbm,
    q_all,
    kv_own,
    gathered_0,
    gathered_1,
    picked,
    arrived_0,
    arrived_1,
    k_aug,
    v_aug,
    q_doc,
    acc_ref,
    top_ref,
    out_all,
    kv_send,
    kv_recv,
    q_send,
    q_recv,
    pre_send,
    pre_recv,
    a_send,
    a_recv,
    b_send,
    b_recv,
    o_send,
    o_recv,
    local_kv,
    local_q,
    local_g,
    local_o,
):
    block = NY * rows
    half = block // 2
    gathered, arrived = (gathered_0, gathered_1), (arrived_0, arrived_1)
    blk, uly = lax.axis_index("blk"), lax.axis_index("uly")
    xh, z, c = blk // 8, (blk // 2) % 4, blk % 2
    xl, y = uly // NY, uly % NY
    x = xh * 2 + xl
    a = x * (1 - c) + z * c
    b = z * (1 - c) + x * c
    a_other = z * (1 - c) + x * c
    partner = device(x, y, z, 1 - c)

    def along_a(a_to):
        return device(a_to * (1 - c) + x * c, y, z * (1 - c) + a_to * c, c)

    def along_b(b_to, c_to):
        return device(x * (1 - c) + b_to * c, y, b_to * (1 - c) + z * c, c_to)

    def remote(src, dst, send, recv, to):
        return pltpu.make_async_remote_copy(
            src_ref=src, dst_ref=dst, send_sem=send, recv_sem=recv, device_id=to, device_id_type=MESH
        )

    barrier = pltpu.get_barrier_semaphore()
    friends = [partner] + [device(x, (y + k) % 4, z, c) for k in (1, 2, 3)]
    for k in (1, 2, 3):
        for core in (0, 1):
            friends.append(device((x + k) % 4, y, z, core))
            friends.append(device(x, y, (z + k) % 4, core))
    for friend in friends:
        pl.semaphore_signal(barrier, inc=1, device_id=friend, device_id_type=MESH)
    pl.semaphore_wait(barrier, len(friends))

    def kv_copy(h, kv, k):
        to = (y + k) % 4
        columns = pl.ds(pl.multiple_of((to * HEADS + h) * HD, HD), HD)
        src = (k_hbm if kv == 0 else v_hbm).at[:, columns]
        dst = kv_own.at[h, kv, pl.ds(pl.multiple_of(y * rows, rows), rows)]
        if k == 0:
            return pltpu.make_async_copy(src, dst, local_kv.at[h, kv])
        return remote(src, dst, kv_send.at[h, kv, k - 1], kv_recv.at[h, kv, k - 1], device(x, to, z, c))

    def q_copy(h, k):
        to = (y + k) % 4
        width = GROUP * HD
        columns = pl.ds(pl.multiple_of((to * HEADS + h) * width, width), width)
        src, dst = q_hbm.at[:, columns], q_all.at[h, y]
        if k == 0:
            return pltpu.make_async_copy(src, dst, local_q.at[h])
        return remote(src, dst, q_send.at[h, k - 1], q_recv.at[h, k - 1], device(x, to, z, c))

    def out_copy(h, t, k):
        width = GROUP * HD
        columns = pl.ds(pl.multiple_of((y * HEADS + h) * width, width), width)
        src, dst = out_all.at[h, t], out_hbm.at[:, columns]
        if k == 0:
            return pltpu.make_async_copy(src, dst, local_o.at[h])
        return remote(src, dst, o_send.at[h, k - 1], o_recv.at[h, k - 1], device(x, t, z, c))

    my_rows = pl.ds(pl.multiple_of(c * half, half), half)
    other_rows = pl.ds(pl.multiple_of((1 - c) * half, half), half)

    def pre_copy(h):
        return remote(
            kv_own.at[h, :, other_rows],
            gathered[h].at[a_other * 2 + c],
            pre_send.at[h],
            pre_recv.at[h],
            partner,
        )

    def own_half(h):
        return pltpu.make_async_copy(kv_own.at[h, :, my_rows], gathered[h].at[a * 2 + c], local_g.at[h])

    def a_copy(h, own, k):
        slot = a * 2 + (c if own else 1 - c)
        src = kv_own.at[h, :, my_rows] if own else gathered[h].at[slot]
        index = 0 if own else 1
        return remote(
            src,
            gathered[h].at[slot],
            a_send.at[h, index, k - 1],
            a_recv.at[h, index, k - 1],
            along_a((a + k) % 4),
        )

    def b_copy(h, core, k):
        return remote(
            picked.at[h, core, k],
            arrived[h].at[c, b],
            b_send.at[h, core, k],
            b_recv.at[h, c, k],
            along_b((b + k) % 4, core),
        )

    def b_partner(h):
        return remote(
            picked.at[h, 0, 0],
            arrived[h].at[c, b],
            b_send.at[h, 0, 0],
            b_recv.at[h, c, 0],
            partner,
        )

    def b_wait(h, r, k):
        slot = ((z if r == 0 else x) - k + 4) % 4
        remote(
            picked.at[h, 0, 0],
            arrived[h].at[r, slot],
            b_send.at[h, 0, 0],
            b_recv.at[h, r, k],
            partner,
        ).wait_recv()

    def wanted(x_to, z_to, c_to, h):
        place = (x_to // 2) * 16 + z_to * 4 + c_to * 2 + x_to % 2
        pick = selected[place, y * HEADS + h]
        return pick, (pick // 16) * 2 + pick % 2, (pick // 4) % 4, (pick // 2) % 2

    def choose(h, x_to, z_to, c_to):
        _, x_s, z_s, c_s = wanted(x_to, z_to, c_to, h)
        return gathered[h][(x_s * (1 - c) + z_s * c) * 2 + c_s]

    lane = lax.broadcasted_iota(jnp.int32, (1, HD), 1)
    begin = jnp.zeros((1, HD), jnp.int32)
    end = jnp.full((1, HD), 1 << 30, jnp.int32)
    total = jnp.int32(0)
    for d in range(4):
        begin = jnp.where(lane == d, total, begin)
        total = total + lengths[d]
        end = jnp.where(lane == d, total, end)

    place_me = xh * 16 + z * 4 + c * 2 + xl

    def inside(first, n):
        p = first + lax.broadcasted_iota(jnp.int32, (n, HD), 0)
        return (p >= begin) & (p < end)

    def penalty(first, n, live):
        visible = inside(first, n)
        hidden = jnp.where(live, 0.0, -BIG)
        return jnp.where(visible, hidden, -BIG).astype(jnp.bfloat16)

    def scores(q_tile, keys):
        return lax.dot_general(
            q_tile, keys, (((1,), (1,)), ((), ())), preferred_element_type=jnp.float32
        )

    def query(h, t, j):
        return jnp.concatenate(
            [q_all[h, t, :, j * HD : (j + 1) * HD], q_doc[pl.ds(pl.multiple_of(t * rows, rows), rows)]], axis=1
        )

    def own_setup(h):
        k_aug[h, 0, :, :HD] = kv_own[h, 0]
        k_aug[h, 0, :, HD:] = penalty(place_me * block, block, True)
        v_aug[h, 0, :, :HD] = kv_own[h, 1]
        v_aug[h, 0, :, HD:] = jnp.ones((block, HD), jnp.bfloat16)

    def own_attention(h):
        row = lax.broadcasted_iota(jnp.int32, (rows, rows), 0)
        column = lax.broadcasted_iota(jnp.int32, (rows, rows), 1)
        for t in range(NY):
            for j in range(GROUP):
                q_tile = query(h, t, j)
                last = scores(q_tile, k_aug[h, 0, t * rows : (t + 1) * rows])
                last = jnp.where(row >= column, last, -BIG)
                top = jnp.max(last, axis=1, keepdims=True)
                if t > 0:
                    first = scores(q_tile, k_aug[h, 0, : t * rows])
                    top = jnp.maximum(top, jnp.max(first, axis=1, keepdims=True))
                weight = jnp.exp2((last - top) * LOG2E_SCALE).astype(jnp.bfloat16)
                acc = jnp.dot(
                    weight, v_aug[h, 0, t * rows : (t + 1) * rows], preferred_element_type=jnp.float32
                )
                if t > 0:
                    weight = jnp.exp2((first - top) * LOG2E_SCALE).astype(jnp.bfloat16)
                    acc = acc + jnp.dot(weight, v_aug[h, 0, : t * rows], preferred_element_type=jnp.float32)
                acc_ref[h, t, j] = acc
                top_ref[h, t, j] = jnp.broadcast_to(top, (rows, HD))

    def sel_setup(h):
        pick, x_s, z_s, _ = wanted(x, z, c, h)
        live = pick != place_me
        for r, slot in ((0, z_s), (1, x_s)):
            there = slice(r * half, (r + 1) * half)
            both = arrived[h][r, slot]
            k_aug[h, 1, there, :HD] = both[0]
            k_aug[h, 1, there, HD:] = penalty(pick * block + r * half, half, live)
            v_aug[h, 1, there, :HD] = both[1]
            v_aug[h, 1, there, HD:] = jnp.ones((half, HD), jnp.bfloat16)

    def sel_attention(h, t):
        for j in range(GROUP):
            s = scores(query(h, t, j), k_aug[h, 1])
            before = top_ref[h, t, j][:, :1]
            top = jnp.maximum(before, jnp.max(s, axis=1, keepdims=True))
            weight = jnp.exp2((s - top) * LOG2E_SCALE).astype(jnp.bfloat16)
            acc = jnp.dot(weight, v_aug[h, 1], preferred_element_type=jnp.float32)
            acc = acc + acc_ref[h, t, j] * jnp.exp2((before - top) * LOG2E_SCALE)
            out_all[h, t, :, j * HD : (j + 1) * HD] = (acc[:, :HD] / acc[:, HD:]).astype(jnp.bfloat16)

    for h in range(HEADS):
        for k in (2, 1, 3, 0):
            for kv in (0, 1):
                kv_copy(h, kv, k).start()
    for h in range(HEADS):
        for k in (2, 1, 3, 0):
            q_copy(h, k).start()
    q_doc[...] = jnp.where(inside(place_me * block, block), 1.0, 0.0).astype(jnp.bfloat16)

    for h in range(HEADS):
        for kv in (0, 1):
            kv_copy(h, kv, 0).wait()
            for k in (1, 2, 3):
                kv_copy(h, kv, k).wait_recv()
        pre_copy(h).start()
        for k in (2, 1, 3):
            a_copy(h, True, k).start()
        own_half(h).start()
        own_setup(h)
        pre_copy(h).wait_recv()
        for k in (2, 1, 3):
            a_copy(h, False, k).start()

    for h in range(HEADS):
        own_half(h).wait()
        for index in (True, False):
            for k in (1, 2, 3):
                a_copy(h, index, k).wait_recv()
        for k in (2, 1, 3):
            b_to = (b + k) % 4
            for core in (0, 1):
                picked[h, core, k] = choose(h, x * (1 - c) + b_to * c, b_to * (1 - c) + z * c, core)
                b_copy(h, core, k).start()
        picked[h, 0, 0] = choose(h, x, z, 1 - c)
        b_partner(h).start()
        arrived[h][c, b] = choose(h, x, z, c)
        q_copy(h, 0).wait()
        for k in (1, 2, 3):
            q_copy(h, k).wait_recv()
        own_attention(h)

    for h in range(HEADS):
        for k in (1, 2, 3):
            b_wait(h, 0, k)
            b_wait(h, 1, k)
        b_back = remote(
            picked.at[h, 0, 0],
            arrived[h].at[1 - c, z * c + x * (1 - c)],
            b_send.at[h, 0, 0],
            b_recv.at[h, 1 - c, 0],
            partner,
        )
        b_back.wait_recv()
        sel_setup(h)
        for k in (2, 1, 3, 0):
            t = (y + k) % 4
            sel_attention(h, t)
            out_copy(h, t, k).start()

    for h in range(HEADS):
        for k in (1, 2, 3):
            for kv in (0, 1):
                kv_copy(h, kv, k).wait_send()
            q_copy(h, k).wait_send()
            a_copy(h, True, k).wait_send()
            a_copy(h, False, k).wait_send()
            b_copy(h, 0, k).wait_send()
            b_copy(h, 1, k).wait_send()
        pre_copy(h).wait_send()
        b_partner(h).wait_send()
        out_copy(h, y, 0).wait()
        for k in (1, 2, 3):
            out_copy(h, (y + k) % 4, k).wait_send()
            out_copy(h, (y + k) % 4, k).wait_recv()


def on_device(queries, keys, values, doc_lengths, selected):
    rows = queries.shape[0]
    block = NY * rows
    half = block // 2
    width = GROUP * HD
    bf16, f32 = jnp.bfloat16, jnp.float32
    dma = pltpu.SemaphoreType.DMA
    anywhere = pl.BlockSpec(memory_space=pl.ANY)
    scalars = pl.BlockSpec(memory_space=pltpu.SMEM)
    return pl.pallas_call(
        functools.partial(kernel, rows),
        out_shape=jax.ShapeDtypeStruct(queries.shape, bf16),
        in_specs=[anywhere, anywhere, anywhere, scalars, scalars],
        out_specs=anywhere,
        scratch_shapes=[
            pltpu.VMEM((HEADS, NY, rows, width), bf16),
            pltpu.VMEM((HEADS, 2, block, HD), bf16),
            pltpu.VMEM((8, 2, half, HD), bf16),
            pltpu.VMEM((8, 2, half, HD), bf16),
            pltpu.VMEM((HEADS, 2, 4, 2, half, HD), bf16),
            pltpu.VMEM((2, 4, 2, half, HD), bf16),
            pltpu.VMEM((2, 4, 2, half, HD), bf16),
            pltpu.VMEM((HEADS, 2, block, 2 * HD), bf16),
            pltpu.VMEM((HEADS, 2, block, 2 * HD), bf16),
            pltpu.VMEM((block, HD), bf16),
            pltpu.VMEM((HEADS, NY, GROUP, rows, 2 * HD), f32),
            pltpu.VMEM((HEADS, NY, GROUP, rows, HD), f32),
            pltpu.VMEM((HEADS, NY, rows, width), bf16),
            dma((HEADS, 2, 3)),
            dma((HEADS, 2, 3)),
            dma((HEADS, 3)),
            dma((HEADS, 3)),
            dma((HEADS,)),
            dma((HEADS,)),
            dma((HEADS, 2, 3)),
            dma((HEADS, 2, 3)),
            dma((HEADS, 2, 4)),
            dma((HEADS, 2, 4)),
            dma((HEADS, 3)),
            dma((HEADS, 3)),
            dma((HEADS, 2)),
            dma((HEADS,)),
            dma((HEADS,)),
            dma((HEADS,)),
        ],
        compiler_params=pltpu.CompilerParams(
            collective_id=0, has_side_effects=True, vmem_limit_bytes=60 * 1024 * 1024
        ),
        name="exchange_and_attend",
    )(queries, keys, values, doc_lengths, selected)


def solution(mesh):
    rows = P(("blk", "uly"), None)
    return jax.shard_map(
        on_device, mesh=mesh, in_specs=(rows, rows, rows, P(), P()), out_specs=rows, check_vma=False
    )
```

time: 341 us -> 88.5 us (0.26)
  waiting for transfers between devices: 109 us -> 0 us
  Pallas kernels: 0 us -> 83.8 us
  local copies, waits for them, and re-layouts: 69.4 us -> 4.49 us
  matrix products: 57.4 us -> 0 us
  blocking collectives: 54.8 us -> 0 us
  other arithmetic: 27.3 us -> 0 us
  between operations: 13.5 us -> 0.01 us
  loops' own time: 3.8 us -> 0 us
  starting transfers between devices: 3.65 us -> 0 us
    all_gather x2 -> x0, waiting for transfers between devices: 85.8 us -> none  [the longest x1 50.9 us: on_device(): k_piece = lax.all_gather(k_heads, 'blk', axis=0, tiled=True)]
    pallas_call x0 -> x1, Pallas kernels: none -> 83.8 us  [on_device(): pl.pallas_call(functools.partial(kernel, rows), out_shape=jax.ShapeDtypeS...]
    dot_general x8 -> x0, matrix products: 57.4 us -> none  [the longest x2 21.9 us: one_block(): jnp.einsum('gmn,nd->mgd', sel_weight.astype(jnp.bfloat16), chosen_v[row,...]
    all_to_all x3 -> x0, blocking collectives: 54.8 us -> none  [the longest x1 29.8 us: on_device(): lax.all_to_all(shortened(head_major), 'uly', split_axis=0, concat_axis=1,...]
    gather x4 -> x0, local copies, waits for them, and re-layouts: 45.6 us -> none  [the longest x2 22.9 us: on_device(): v_got = v_piece.reshape(count, kv_dev, HD)[index, head_rows]]
    all_to_all x1 -> x0, waiting for transfers between devices: 22.7 us -> none  [on_device(): lax.all_to_all(queries, 'uly', split_axis=1, concat_axis=0, tiled=True)]
    reduce_sum x4 -> x0, other arithmetic: 20.1 us -> none  [the longest x2 19.9 us: one_block(): total = jnp.sum(own_weight, axis=-1) + jnp.sum(sel_weight, axis=-1)]
    all_to_all x5 -> x0, local copies, waits for them, and re-layouts: 10.8 us -> none  [the longest x2 6.44 us: on_device(): lax.all_to_all(shortened(head_major), 'uly', split_axis=0, concat_axis=1,...]
  transfers between devices with their start and end apart: 3 -> 0, of which waited for: 3 -> 0; matrix products, arithmetic and copies ran while one was open for 9% -> 0% of each run, Pallas kernels for 0% -> 0%
where the time goes in v1:
time: 88.5 us; the launch traced here: 88.3 us
  Pallas kernels  83.8 us (95%)
  local copies, waits for them, and re-layouts  4.49 us (5%)
    pallas_call x1, Pallas kernels, on_device(): pl.pallas_call(functools.partial(kernel, rows), out_shape=jax.ShapeDtypeS...  83.8 us
    unnamed x2, local copies, waits for them, and re-layouts  4.49 us

profile of v1, /device:TPU:1, one launch (start us, length us, event | category | flops | bytes accessed | tf_op | source)
XLA Modules:
  0.0 88.3 jit_solution(1782446675457898920)
XLA Ops:
  0.0 1.4 %copy.6.selected = s32[32,8]{1,0:T(8,128)} copy(s32[32,8]{0,1:T(8,128)} %param.9) | data formatting | bytes 2048 | tf_op args[4]
  1.4 83.8 %exchange_and_attend.1 = bf16[256,4096]{1,0:T(8,128)(2,1)} custom-call(bf16[256,4096]{1,0:T(8,128)(2,1)} %q_hbm.1, bf16[256,1024]{1,0:T(8,128)(2,1)} %k_hbm.1, bf16[256,1024]{1,0:T(8,128)(2,1)} %v_hbm.1, s32[4]{0:T(128)} %lengths.1, s32[32,8]{1,0:T(8,128)} %copy.6.selected), custom_call_target="tpu_custom_call" | custom-call | tf_op jit(solution)/shard_map/exchange_and_attend/pallas_call | solution.py:351
  85.2 3.1 %copy.8 = bf16[256,4096]{1,0:T(8,128)(2,1)} copy(bf16[256,4096]{1,0:T(8,128)(2,1)} %exchange_and_attend.1) | data formatting | bytes 4194304

commit v2 on v1

v2 whole, which is shorter than its diff:
```python
import functools
import math

import jax
import jax.numpy as jnp
from jax import lax
from jax.experimental import pallas as pl
from jax.experimental.pallas import tpu as pltpu
from jax.sharding import PartitionSpec as P

HQ = 32
KVH = 8
HD = 128
NY = 4
GROUP = HQ // KVH
HEADS = KVH // NY
BIG = float(1 << 20)
LOG2E_SCALE = math.log2(math.e) / math.sqrt(HD)
MESH = pl.DeviceIdType.MESH


def device(x, y, z, c):
    return ((x // 2) * 8 + z * 2 + c, (x % 2) * NY + y)


def kernel(
    rows,
    q_hbm,
    k_hbm,
    v_hbm,
    lengths,
    selected,
    out_hbm,
    q_all,
    kv_own,
    gathered_00,
    gathered_01,
    gathered_10,
    gathered_11,
    relayed_00,
    relayed_01,
    relayed_10,
    relayed_11,
    picked,
    final,
    arrived_0,
    arrived_1,
    k_aug,
    v_aug,
    q_doc,
    acc_ref,
    top_ref,
    out_all,
    kv_send,
    kv_recv,
    q_send,
    q_recv,
    pre_send,
    pre_recv,
    a_send,
    a_recv,
    b_send,
    b_recv,
    c_recv,
    o_send,
    o_recv,
    local_kv,
    local_q,
    local_g,
    local_o,
):
    block = NY * rows
    quarter = rows // 4
    gathered = ((gathered_00, gathered_01), (gathered_10, gathered_11))
    relayed = ((relayed_00, relayed_01), (relayed_10, relayed_11))
    arrived = (arrived_0, arrived_1)
    blk, uly = lax.axis_index("blk"), lax.axis_index("uly")
    xh, z, c = blk // 8, (blk // 2) % 4, blk % 2
    xl, y = uly // NY, uly % NY
    x = xh * 2 + xl
    a = x * (1 - c) + z * c
    b = z * (1 - c) + x * c
    partner = device(x, y, z, 1 - c)

    def along_a(a_to):
        return device(a_to * (1 - c) + x * c, y, z * (1 - c) + a_to * c, c)

    def along_b(b_to, c_to):
        return device(x * (1 - c) + b_to * c, y, b_to * (1 - c) + z * c, c_to)

    def remote(src, dst, send, recv, to):
        return pltpu.make_async_remote_copy(
            src_ref=src, dst_ref=dst, send_sem=send, recv_sem=recv, device_id=to, device_id_type=MESH
        )

    barrier = pltpu.get_barrier_semaphore()
    friends = [partner] + [device(x, (y + k) % 4, z, c) for k in (1, 2, 3)]
    for k in (1, 3):
        for core in (0, 1):
            friends.append(device((x + k) % 4, y, z, core))
            friends.append(device(x, y, (z + k) % 4, core))
    for friend in friends:
        pl.semaphore_signal(barrier, inc=1, device_id=friend, device_id_type=MESH)

    def kv_copy(h, kv, k):
        to = (y + k) % 4
        columns = pl.ds(pl.multiple_of((to * HEADS + h) * HD, HD), HD)
        src = (k_hbm if kv == 0 else v_hbm).at[:, :, columns]
        dst = kv_own.at[h, :, kv, y]
        if k == 0:
            return pltpu.make_async_copy(src, dst, local_kv.at[h, kv])
        return remote(src, dst, kv_send.at[h, kv, k - 1], kv_recv.at[h, kv, k - 1], device(x, to, z, c))

    def q_copy(h, k):
        to = (y + k) % 4
        width = GROUP * HD
        columns = pl.ds(pl.multiple_of((to * HEADS + h) * width, width), width)
        src, dst = q_hbm.at[:, columns], q_all.at[h, y]
        if k == 0:
            return pltpu.make_async_copy(src, dst, local_q.at[h])
        return remote(src, dst, q_send.at[h, k - 1], q_recv.at[h, k - 1], device(x, to, z, c))

    def out_copy(h, t, k):
        width = GROUP * HD
        columns = pl.ds(pl.multiple_of((y * HEADS + h) * width, width), width)
        src, dst = out_all.at[h, t], out_hbm.at[:, columns]
        if k == 0:
            return pltpu.make_async_copy(src, dst, local_o.at[h])
        return remote(src, dst, o_send.at[h, k - 1], o_recv.at[h, k - 1], device(x, t, z, c))

    def near(p):
        return p + 1 - 2 * (p % 2)

    def far(p):
        return 3 - p

    def pairing(j, step):
        return (near, far)[(j + step) % 2]

    def source(k):
        return (y - k + 4) % 4

    def pre_copy(h, j, k):
        chunk = source(k)
        return remote(
            kv_own.at[h, 2 * (1 - c) + j, :, chunk],
            gathered[h][j].at[b * 2 + c, :, chunk],
            pre_send.at[h, j, k],
            pre_recv.at[h, j, k],
            partner,
        )

    def own_item(h, j):
        return pltpu.make_async_copy(kv_own.at[h, 2 * c + j], gathered[h][j].at[a * 2 + c], local_g.at[h, j])

    def first_copy(h, j, own, k=None):
        slot = a * 2 + (c if own else 1 - c)
        src = kv_own.at[h, 2 * c + j] if own else gathered[h][j].at[slot]
        dst = gathered[h][j].at[slot]
        if k is not None:
            src, dst = src.at[:, source(k)], dst.at[:, source(k)]
        index = 0 if own else 1
        return remote(
            src,
            dst,
            a_send.at[h, j, index],
            a_recv.at[h, j, index],
            along_a(pairing(j, 0)(a)),
        )

    def second_copy(h, j, own):
        place = a if own else pairing(j, 0)(a)
        pair = pl.ds(place * 2, 2)
        index = 2 if own else 3
        return remote(
            gathered[h][j].at[pair],
            gathered[h][j].at[pair],
            a_send.at[h, j, index],
            a_recv.at[h, j, index],
            along_a(pairing(j, 1)(a)),
        )

    def third_copy(h, j):
        return remote(
            picked.at[h, j], relayed[h][j], b_send.at[h, j, 0], b_recv.at[h, j, 0], along_b(pairing(j, 0)(b), c)
        )

    def fourth_copy(h, j, core):
        return remote(
            final.at[h, j, core],
            arrived[h].at[2 * c + j, 1],
            b_send.at[h, j, 1 + core],
            c_recv.at[h, 2 * c + j, 1],
            along_b(pairing(j, 1)(b), core),
        )

    def partner_copy(h, j):
        return remote(
            final.at[h, j, 2],
            arrived[h].at[2 * c + j, 0],
            b_send.at[h, j, 3],
            c_recv.at[h, 2 * c + j, 0],
            partner,
        )

    def arrival(h, unit, slot):
        return remote(
            final.at[h, 0, 0], arrived[h].at[unit, slot], b_send.at[h, 0, 1], c_recv.at[h, unit, slot], partner
        )

    def wanted(x_to, z_to, c_to, h):
        place = (x_to // 2) * 16 + z_to * 4 + c_to * 2 + x_to % 2
        pick = selected[y * HEADS + h, place]
        return pick, (pick // 16) * 2 + pick % 2, (pick // 4) % 4, (pick // 2) % 2

    def request(h, b_to, c_to):
        x_to, z_to = x * (1 - c) + b_to * c, b_to * (1 - c) + z * c
        _, x_s, z_s, c_s = wanted(x_to, z_to, c_to, h)
        return (x_s * (1 - c) + z_s * c) * 2 + c_s, z_s * (1 - c) + x_s * c

    def pick_third(h, j):
        to = pairing(j, 0)(b)
        for w, b_to in ((0, to), (1, pairing(j, 1)(to))):
            for core in (0, 1):
                picked[h, j, 2 * w + core] = gathered[h][j][request(h, b_to, core)[0]]

    def pick_fourth(h, j, w, core):
        b_to = pairing(j, 1)(b) if w else b
        index, b_s = request(h, b_to, core)
        return jnp.where(b_s == b, gathered[h][j][index], relayed[h][j][2 * w + core])

    lane = lax.broadcasted_iota(jnp.int32, (1, HD), 1)
    begin = jnp.zeros((1, HD), jnp.int32)
    end = jnp.full((1, HD), 1 << 30, jnp.int32)
    total = jnp.int32(0)
    for d in range(4):
        begin = jnp.where(lane == d, total, begin)
        total = total + lengths[d]
        end = jnp.where(lane == d, total, end)

    place_me = xh * 16 + z * 4 + c * 2 + xl

    def inside(first, n):
        p = first + lax.broadcasted_iota(jnp.int32, (n, HD), 0)
        return (p >= begin) & (p < end)

    def penalty(first, live, regrouped):
        i = lax.broadcasted_iota(jnp.int32, (block, HD), 0)
        if regrouped:
            i = (i // quarter % NY) * rows + (i // rows) * quarter + i % quarter
        p = first + i
        visible = (p >= begin) & (p < end)
        hidden = jnp.where(live, 0.0, -BIG)
        return jnp.where(visible, hidden, -BIG).astype(jnp.bfloat16)

    def scores(q_tile, keys):
        return lax.dot_general(
            q_tile, keys, (((1,), (1,)), ((), ())), preferred_element_type=jnp.float32
        )

    def query(h, t, j):
        return jnp.concatenate(
            [q_all[h, t, :, j * HD : (j + 1) * HD], q_doc[pl.ds(pl.multiple_of(t * rows, rows), rows)]], axis=1
        )

    def own_setup(h):
        for chunk in range(NY):
            for unit in range(4):
                there = slice(chunk * rows + unit * quarter, chunk * rows + (unit + 1) * quarter)
                k_aug[h, 0, there, :HD] = kv_own[h, unit, 0, chunk]
                v_aug[h, 0, there, :HD] = kv_own[h, unit, 1, chunk]
        k_aug[h, 0, :, HD:] = penalty(place_me * block, True, False)
        v_aug[h, 0, :, HD:] = jnp.ones((block, HD), jnp.bfloat16)

    def own_attention(h, tiles):
        row = lax.broadcasted_iota(jnp.int32, (rows, rows), 0)
        column = lax.broadcasted_iota(jnp.int32, (rows, rows), 1)
        for t in tiles:
            for j in range(GROUP):
                q_tile = query(h, t, j)
                last = scores(q_tile, k_aug[h, 0, t * rows : (t + 1) * rows])
                last = jnp.where(row >= column, last, -BIG)
                top = jnp.max(last, axis=1, keepdims=True)
                if t > 0:
                    first = scores(q_tile, k_aug[h, 0, : t * rows])
                    top = jnp.maximum(top, jnp.max(first, axis=1, keepdims=True))
                weight = jnp.exp2((last - top) * LOG2E_SCALE).astype(jnp.bfloat16)
                acc = jnp.dot(
                    weight, v_aug[h, 0, t * rows : (t + 1) * rows], preferred_element_type=jnp.float32
                )
                if t > 0:
                    weight = jnp.exp2((first - top) * LOG2E_SCALE).astype(jnp.bfloat16)
                    acc = acc + jnp.dot(weight, v_aug[h, 0, : t * rows], preferred_element_type=jnp.float32)
                acc_ref[h, t, j] = acc
                top_ref[h, t, j] = jnp.broadcast_to(top, (rows, HD))

    def sel_setup(h):
        pick, x_s, z_s, _ = wanted(x, z, c, h)
        live = pick != place_me
        for r, source, here in ((0, z_s, z), (1, x_s, x)):
            for j in (0, 1):
                unit = 2 * r + j
                slot = jnp.where((source == here) | (source == pairing(j, 0)(here)), 0, 1)
                both = arrived[h][unit, slot]
                there = slice(unit * rows, (unit + 1) * rows)
                k_aug[h, 1, there, :HD] = both[0].reshape(rows, HD)
                v_aug[h, 1, there, :HD] = both[1].reshape(rows, HD)
        k_aug[h, 1, :, HD:] = penalty(pick * block, live, True)
        v_aug[h, 1, :, HD:] = jnp.ones((block, HD), jnp.bfloat16)

    def sel_attention(h, t):
        for j in range(GROUP):
            s = scores(query(h, t, j), k_aug[h, 1])
            before = top_ref[h, t, j][:, :1]
            top = jnp.maximum(before, jnp.max(s, axis=1, keepdims=True))
            weight = jnp.exp2((s - top) * LOG2E_SCALE).astype(jnp.bfloat16)
            acc = jnp.dot(weight, v_aug[h, 1], preferred_element_type=jnp.float32)
            acc = acc + acc_ref[h, t, j] * jnp.exp2((before - top) * LOG2E_SCALE)
            out_all[h, t, :, j * HD : (j + 1) * HD] = (acc[:, :HD] / acc[:, HD:]).astype(jnp.bfloat16)

    for h in range(HEADS):
        for kv in (0, 1):
            kv_copy(h, kv, 0).start()
    for h in range(HEADS):
        q_copy(h, 0).start()
    q_doc[...] = jnp.where(inside(place_me * block, block), 1.0, 0.0).astype(jnp.bfloat16)
    pl.semaphore_wait(barrier, len(friends))

    def send_keys(h):
        for k in (1, 3, 2):
            for kv in (0, 1):
                if h > 0:
                    kv_copy(h - 1, kv, k).wait_send()
                kv_copy(h, kv, k).start()

    def send_queries(h):
        for k in (1, 3, 2):
            if h == 0:
                for kv in (0, 1):
                    kv_copy(HEADS - 1, kv, k).wait_send()
            else:
                q_copy(h - 1, k).wait_send()
            q_copy(h, k).start()

    def send_first(h, k):
        for kv in (0, 1):
            if k == 0:
                kv_copy(h, kv, k).wait()
            else:
                kv_copy(h, kv, k).wait_recv()
        for j in (0, 1):
            pre_copy(h, j, k).start()
        for j in (0, 1):
            first_copy(h, j, True, k).start()

    def pass_first(h, k):
        for j in (0, 1):
            pre_copy(h, j, k).wait_recv()
            first_copy(h, j, False, k).start()

    def send_second_own(h):
        for j in (0, 1):
            own_item(h, j).start()
        for j in (0, 1):
            own_item(h, j).wait()
            second_copy(h, j, True).start()

    def send_second(h):
        for j in (0, 1):
            first_copy(h, j, True).wait_recv()
            first_copy(h, j, False).wait_recv()
            second_copy(h, j, False).start()

    def send_third(h):
        for j in (0, 1):
            second_copy(h, j, True).wait_recv()
            second_copy(h, j, False).wait_recv()
            pick_third(h, j)
            third_copy(h, j).start()

    def send_fourth(h):
        for j in (0, 1):
            third_copy(h, j).wait_recv()
            for core in (0, 1):
                final[h, j, core] = pick_fourth(h, j, 1, core)
                fourth_copy(h, j, core).start()
        for j in (0, 1):
            final[h, j, 2] = jnp.where(c == 0, pick_fourth(h, j, 0, 1), pick_fourth(h, j, 0, 0))
            partner_copy(h, j).start()
            arrived[h][2 * c + j, 0] = jnp.where(c == 0, pick_fourth(h, j, 0, 0), pick_fourth(h, j, 0, 1))

    def queries_here(h):
        q_copy(h, 0).wait()
        for k in (1, 2, 3):
            q_copy(h, k).wait_recv()

    def finish(h):
        for unit in range(4):
            arrival(h, unit, 1).wait_recv()
        for j in (0, 1):
            arrival(h, 2 * (1 - c) + j, 0).wait_recv()
        sel_setup(h)
        for k in (2, 1, 3, 0):
            t = (y + k) % 4
            sel_attention(h, t)
            out_copy(h, t, k).start()

    send_keys(0)
    for h in range(HEADS):
        send_first(h, 0)
    for h in range(HEADS):
        pass_first(h, 0)
    send_keys(1)
    for k in (1, 3, 2):
        send_first(0, k)
        pass_first(0, k)
    send_second_own(0)
    send_queries(0)
    own_setup(0)
    send_second(0)
    for k in (1, 3, 2):
        send_first(1, k)
        pass_first(1, k)
    send_second_own(1)
    own_setup(1)
    send_third(0)
    send_queries(1)
    for j in (0, 1):
        third_copy(0, j).wait_send()
    send_second(1)
    queries_here(0)
    own_attention(0, (0, 1))
    send_fourth(0)
    own_attention(0, (2, 3))
    send_third(1)
    finish(0)
    queries_here(1)
    own_attention(1, (0, 1, 2))
    send_fourth(1)
    own_attention(1, (3,))
    finish(1)

    for h in range(HEADS):
        for j in (0, 1):
            for k in range(NY):
                pre_copy(h, j, k).wait_send()
            for own in (True, False):
                first_copy(h, j, own).wait_send()
                second_copy(h, j, own).wait_send()
            if h > 0:
                third_copy(h, j).wait_send()
            for core in (0, 1):
                fourth_copy(h, j, core).wait_send()
            partner_copy(h, j).wait_send()
        out_copy(h, y, 0).wait()
        for k in (1, 2, 3):
            if h > 0:
                q_copy(h, k).wait_send()
            out_copy(h, (y + k) % 4, k).wait_send()
            out_copy(h, (y + k) % 4, k).wait_recv()


def on_device(queries, keys, values, doc_lengths, selected):
    rows = queries.shape[0]
    block = NY * rows
    item = (2, NY, rows // 4, HD)
    width = GROUP * HD
    split = (4, rows // 4, keys.shape[1])
    bf16, f32 = jnp.bfloat16, jnp.float32
    dma = pltpu.SemaphoreType.DMA
    anywhere = pl.BlockSpec(memory_space=pl.ANY)
    scalars = pl.BlockSpec(memory_space=pltpu.SMEM)
    return pl.pallas_call(
        functools.partial(kernel, rows),
        out_shape=jax.ShapeDtypeStruct(queries.shape, bf16),
        in_specs=[anywhere, anywhere, anywhere, scalars, scalars],
        out_specs=anywhere,
        scratch_shapes=[
            pltpu.VMEM((HEADS, NY, rows, width), bf16),
            pltpu.VMEM((HEADS, 4) + item, bf16),
            *[pltpu.VMEM((8,) + item, bf16)] * 4,
            *[pltpu.VMEM((4,) + item, bf16)] * 4,
            pltpu.VMEM((HEADS, 2, 4) + item, bf16),
            pltpu.VMEM((HEADS, 2, 3) + item, bf16),
            *[pltpu.VMEM((4, 2) + item, bf16)] * 2,
            pltpu.VMEM((HEADS, 2, block, 2 * HD), bf16),
            pltpu.VMEM((HEADS, 2, block, 2 * HD), bf16),
            pltpu.VMEM((block, HD), bf16),
            pltpu.VMEM((HEADS, NY, GROUP, rows, 2 * HD), f32),
            pltpu.VMEM((HEADS, NY, GROUP, rows, HD), f32),
            pltpu.VMEM((HEADS, NY, rows, width), bf16),
            dma((HEADS, 2, 3)),
            dma((HEADS, 2, 3)),
            dma((HEADS, 3)),
            dma((HEADS, 3)),
            dma((HEADS, 2, NY)),
            dma((HEADS, 2, NY)),
            dma((HEADS, 2, 4)),
            dma((HEADS, 2, 4)),
            dma((HEADS, 2, 4)),
            dma((HEADS, 2, 1)),
            dma((HEADS, 4, 2)),
            dma((HEADS, 3)),
            dma((HEADS, 3)),
            dma((HEADS, 2)),
            dma((HEADS,)),
            dma((HEADS, 2)),
            dma((HEADS,)),
        ],
        compiler_params=pltpu.CompilerParams(
            collective_id=0, has_side_effects=True, vmem_limit_bytes=60 * 1024 * 1024
        ),
        name="exchange_and_attend",
    )(queries, keys.reshape(split), values.reshape(split), doc_lengths, selected.T)


def solution(mesh):
    rows = P(("blk", "uly"), None)
    return jax.shard_map(
        on_device, mesh=mesh, in_specs=(rows, rows, rows, P(), P()), out_specs=rows, check_vma=False
    )
```

time: 88.5 us -> 80.7 us (0.912)
  Pallas kernels: 83.8 us -> 77.4 us
  local copies, waits for them, and re-layouts: 4.49 us -> 3.13 us
    pallas_call x1, Pallas kernels: 83.8 us -> 77.4 us  [on_device(): pl.pallas_call(functools.partial(kernel, rows), out_shape=jax.ShapeDtypeS...]
    unnamed x2 -> x1, local copies, waits for them, and re-layouts: 4.49 us -> 3.13 us
where the time goes in v2:
time: 80.7 us; the launch traced here: 80.6 us
  Pallas kernels  77.4 us (96%)
  local copies, waits for them, and re-layouts  3.13 us (4%)
    pallas_call x1, Pallas kernels, on_device(): pl.pallas_call(functools.partial(kernel, rows), out_shape=jax.ShapeDtypeS...  77.4 us
    unnamed x1, local copies, waits for them, and re-layouts  3.13 us

profile of v2, /device:TPU:1, one launch (start us, length us, event | category | flops | bytes accessed | tf_op | source)
XLA Modules:
  0.0 80.6 jit_solution(5541325243392984510)
XLA Ops:
  0.0 77.4 %exchange_and_attend.1 = bf16[256,4096]{1,0:T(8,128)(2,1)} custom-call(bf16[256,4096]{1,0:T(8,128)(2,1)} %q_hbm.1, bf16[4,64,1024]{2,1,0:T(8,128)(2,1)} %bitcast.3, bf16[4,64,1024]{2,1,0:T(8,128)(2,1)} %bitcast.4, s32[4]{0:T(128)} %lengths.1, s32[8,32]{1,0:T(8,128)} %bitcast.5), custom_call_target="tpu_custom_call" | custom-call | tf_op jit(solution)/shard_map/exchange_and_attend/pallas_call | solution.py:473
  77.4 3.1 %copy.7 = bf16[256,4096]{1,0:T(8,128)(2,1)} copy(bf16[256,4096]{1,0:T(8,128)(2,1)} %exchange_and_attend.1) | data formatting | bytes 4194304

commit v3 on v2

--- a/solution.py
+++ b/solution.py
@@ -394,33 +394,41 @@
         for k in (1, 2, 3):
             q_copy(h, k).wait_recv()
 
-    def finish(h):
+    def prepare(h):
         for unit in range(4):
             arrival(h, unit, 1).wait_recv()
         for j in (0, 1):
             arrival(h, 2 * (1 - c) + j, 0).wait_recv()
         sel_setup(h)
-        for k in (2, 1, 3, 0):
+
+    def give(h, ks):
+        for k in ks:
             t = (y + k) % 4
             sel_attention(h, t)
             out_copy(h, t, k).start()
 
     send_keys(0)
-    for h in range(HEADS):
-        send_first(h, 0)
-    for h in range(HEADS):
-        pass_first(h, 0)
+    send_first(0, 0)
+    send_first(1, 0)
+    pass_first(0, 0)
+    pass_first(1, 0)
     send_keys(1)
-    for k in (1, 3, 2):
-        send_first(0, k)
-        pass_first(0, k)
+    send_first(0, 1)
+    pass_first(0, 1)
+    send_first(0, 3)
+    pass_first(0, 3)
+    send_first(0, 2)
+    pass_first(0, 2)
     send_second_own(0)
     send_queries(0)
     own_setup(0)
     send_second(0)
-    for k in (1, 3, 2):
-        send_first(1, k)
-        pass_first(1, k)
+    send_first(1, 1)
+    pass_first(1, 1)
+    send_first(1, 3)
+    pass_first(1, 3)
+    send_first(1, 2)
+    pass_first(1, 2)
     send_second_own(1)
     own_setup(1)
     send_third(0)
@@ -429,16 +437,18 @@
         third_copy(0, j).wait_send()
     send_second(1)
     queries_here(0)
-    own_attention(0, (0, 1))
+    own_attention(0, (0, 1,))
     send_fourth(0)
-    own_attention(0, (2, 3))
+    own_attention(0, (2, 3,))
     send_third(1)
-    finish(0)
+    prepare(0)
+    give(0, (2, 1, 3, 0,))
     queries_here(1)
-    own_attention(1, (0, 1, 2))
+    own_attention(1, (0, 1, 2,))
     send_fourth(1)
     own_attention(1, (3,))
-    finish(1)
+    prepare(1)
+    give(1, (2, 1, 3, 0,))
 
     for h in range(HEADS):
         for j in (0, 1):
@@ -472,7 +482,7 @@
     scalars = pl.BlockSpec(memory_space=pltpu.SMEM)
     return pl.pallas_call(
         functools.partial(kernel, rows),
-        out_shape=jax.ShapeDtypeStruct(queries.shape, bf16),
+        out_shape=pltpu.VMEM(queries.shape, bf16),
         in_specs=[anywhere, anywhere, anywhere, scalars, scalars],
         out_specs=anywhere,
         scratch_shapes=[
@@ -508,7 +518,7 @@
             dma((HEADS,)),
         ],
         compiler_params=pltpu.CompilerParams(
-            collective_id=0, has_side_effects=True, vmem_limit_bytes=60 * 1024 * 1024
+            collective_id=0, has_side_effects=True, vmem_limit_bytes=64938 * 1000
         ),
         name="exchange_and_attend",
     )(queries, keys.reshape(split), values.reshape(split), doc_lengths, selected.T)

time: 80.7 us -> 78.8 us (0.976)
  local copies, waits for them, and re-layouts: 3.13 us -> 1.32 us
    unnamed x1, local copies, waits for them, and re-layouts: 3.13 us -> 1.32 us
where the time goes in v3:
time: 78.8 us; the launch traced here: 78.7 us
  Pallas kernels  77.3 us (98%)
  local copies, waits for them, and re-layouts  1.32 us (2%)
    pallas_call x1, Pallas kernels, on_device(): pl.pallas_call(functools.partial(kernel, rows), out_shape=pltpu.VMEM(quer...  77.3 us

profile of v3, /device:TPU:1, one launch (start us, length us, event | category | flops | bytes accessed | tf_op | source)
XLA Modules:
  0.0 78.7 jit_solution(6588048456612483686)
XLA Ops:
  0.0 77.3 %exchange_and_attend.1 = bf16[256,4096]{1,0:T(8,128)(2,1)S(1)} custom-call(bf16[256,4096]{1,0:T(8,128)(2,1)} %q_hbm.1, bf16[4,64,1024]{2,1,0:T(8,128)(2,1)} %bitcast.3, bf16[4,64,1024]{2,1,0:T(8,128)(2,1)} %bitcast.4, s32[4]{0:T(128)} %lengths.1, s32[8,32]{1,0:T(8,128)} %bitcast.5), custom_call_target="tpu_custom_call" | custom-call | tf_op jit(solution)/shard_map/exchange_and_attend/pallas_call | solution.py:483
  77.3 1.3 %copy.7 = bf16[256,4096]{1,0:T(8,128)(2,1)} copy(bf16[256,4096]{1,0:T(8,128)(2,1)S(1)} %exchange_and_attend.1) | data formatting | bytes 4194304

commit v4 on v3

--- a/solution.py
+++ b/solution.py
@@ -271,6 +271,9 @@
                 v_aug[h, 0, there, :HD] = kv_own[h, unit, 1, chunk]
         k_aug[h, 0, :, HD:] = penalty(place_me * block, True, False)
         v_aug[h, 0, :, HD:] = jnp.ones((block, HD), jnp.bfloat16)
+        pick = wanted(x, z, c, h)[0]
+        k_aug[h, 1, :, HD:] = penalty(pick * block, pick != place_me, True)
+        v_aug[h, 1, :, HD:] = jnp.ones((block, HD), jnp.bfloat16)
 
     def own_attention(h, tiles):
         row = lax.broadcasted_iota(jnp.int32, (rows, rows), 0)
@@ -295,8 +298,7 @@
                 top_ref[h, t, j] = jnp.broadcast_to(top, (rows, HD))
 
     def sel_setup(h):
-        pick, x_s, z_s, _ = wanted(x, z, c, h)
-        live = pick != place_me
+        _, x_s, z_s, _ = wanted(x, z, c, h)
         for r, source, here in ((0, z_s, z), (1, x_s, x)):
             for j in (0, 1):
                 unit = 2 * r + j
@@ -305,8 +307,6 @@
                 there = slice(unit * rows, (unit + 1) * rows)
                 k_aug[h, 1, there, :HD] = both[0].reshape(rows, HD)
                 v_aug[h, 1, there, :HD] = both[1].reshape(rows, HD)
-        k_aug[h, 1, :, HD:] = penalty(pick * block, live, True)
-        v_aug[h, 1, :, HD:] = jnp.ones((block, HD), jnp.bfloat16)
 
     def sel_attention(h, t):
         for j in range(GROUP):

time: 78.8 us -> 78.7 us (level)
  no operation moved by 1% of the time
where the time goes in v4:
time: 78.7 us; the launch traced here: 78.6 us
  Pallas kernels  77.2 us (98%)
  local copies, waits for them, and re-layouts  1.32 us (2%)
    pallas_call x1, Pallas kernels, on_device(): pl.pallas_call(functools.partial(kernel, rows), out_shape=pltpu.VMEM(quer...  77.2 us

profile of v4, /device:TPU:1, one launch (start us, length us, event | category | flops | bytes accessed | tf_op | source)
XLA Modules:
  0.0 78.6 jit_solution(6642870075435933803)
XLA Ops:
  0.0 77.2 %exchange_and_attend.1 = bf16[256,4096]{1,0:T(8,128)(2,1)S(1)} custom-call(bf16[256,4096]{1,0:T(8,128)(2,1)} %q_hbm.1, bf16[4,64,1024]{2,1,0:T(8,128)(2,1)} %bitcast.3, bf16[4,64,1024]{2,1,0:T(8,128)(2,1)} %bitcast.4, s32[4]{0:T(128)} %lengths.1, s32[8,32]{1,0:T(8,128)} %bitcast.5), custom_call_target="tpu_custom_call" | custom-call | tf_op jit(solution)/shard_map/exchange_and_attend/pallas_call | solution.py:483
  77.2 1.3 %copy.7 = bf16[256,4096]{1,0:T(8,128)(2,1)} copy(bf16[256,4096]{1,0:T(8,128)(2,1)S(1)} %exchange_and_attend.1) | data formatting | bytes 4194304
